TPU v7x, 32 devices: a whole 2x2x4 slice. The times are simulated.
32 devices in a mesh: shard: 8 (over y, x, core), rep: 4 (over z).
Axes of the slice: x: 2, y: 2, z: 4, core: 2. Of those that a mesh axis runs over, the one named last changes fastest.
Arguments:
- pooled_grad: float32 [128, 4, 8, 256], P('shard', 'rep'), may hold values from -0.8 to 0.8
- bag_lengths: int32 [8, 4, 128], P('shard', 'rep'), may hold values from 1 to 64, 2048 in all within a row
- row_slots: int32 [8, 4, 2048], P('shard', 'rep'), may hold values from 0 to 511
- id_weights: int32 [8, 4, 2048], P('shard', 'rep'), may hold values from 1 to 32
- touched_rows: float32 [8, 512, 256], P('shard'), may hold values from -6 to 6
- accumulator: float32 [8, 512], P('shard'), may hold values from 0.005 to 0.5
Outputs:
- row_grad: float32 [8, 512, 256], P('shard', 'rep')
- updated_rows: float32 [8, 512, 256], P('shard')
Inputs may be any that keep to these rules, and one draw needn't show every extreme that they name: `bag_lengths`: in each table and replica group the bag lengths sum to 2048.
All inputs are finite; a program needn't handle non-finite values.
Results may differ from a plain program's by a relative error of at most 0.0003.
Values sent between devices are 32-bit elements; how exact they have to be, the bound alone decides.
A program may use at most 64 MiB of HBM per device.

v0:
```python
import jax
import jax.numpy as jnp
from jax import lax
from jax.sharding import PartitionSpec as P

learn_rate = 0.5


def table_rows(arrived, lengths, slots, weights, height):
    ends = jnp.cumsum(lengths)
    starts = ends - lengths
    count = slots.shape[0]
    span = min(512, count)
    turns = count // span
    slot_ids = jnp.arange(height, dtype=jnp.int32)

    def add_block(step, total):
        start = step * span
        positions = start + jnp.arange(span, dtype=jnp.int32)
        target = lax.dynamic_slice_in_dim(slots, start, span)
        factor = lax.dynamic_slice_in_dim(weights, start, span)
        chosen = jnp.where(target[:, None] == slot_ids[None, :], factor[:, None], 0).astype(
            jnp.bfloat16
        )
        member = (
            (positions[:, None] >= starts[None, :]) & (positions[:, None] < ends[None, :])
        ).astype(jnp.bfloat16)
        return total + lax.dot_general(
            chosen, member, (((0,), (0,)), ((), ())), preferred_element_type=jnp.float32
        )

    empty = jnp.zeros((height, arrived.shape[0]), jnp.float32)
    tallies = lax.fori_loop(0, turns, add_block, empty)
    return (
        jnp.dot(
            tallies, arrived, precision=lax.Precision.HIGHEST, preferred_element_type=jnp.float32
        )
        * 0.0625
    )


def adagrad(rows, state, grads):
    new_state = state + jnp.mean(grads * grads, axis=-1)
    return rows - learn_rate * grads / (jnp.sqrt(new_state)[..., None] + 1e-08)


def per_device(pooled_grad, bag_lengths, row_slots, id_weights, touched_rows, accumulator):
    arrived = lax.all_to_all(pooled_grad, "shard", split_axis=2, concat_axis=0, tiled=True)
    height = touched_rows.shape[1]
    owned = touched_rows.shape[0]
    local = jnp.stack(
        [table_rows(arrived[:, 0, 0], bag_lengths[0, 0], row_slots[0, 0], id_weights[0, 0], height)]
    )
    count = height // lax.axis_size("rep")
    start = lax.axis_index("rep") * count
    grad_part = lax.psum_scatter(local, "rep", scatter_dimension=1, tiled=True)
    rows_part = lax.dynamic_slice_in_dim(touched_rows, start, count, 1)
    state_part = lax.dynamic_slice_in_dim(accumulator, start, count, 1)
    fresh = adagrad(rows_part, state_part, grad_part)
    updated = lax.all_gather(fresh, "rep", axis=1, tiled=True)
    return (grad_part, updated)


def solution(mesh):
    placed = (
        P("shard", "rep", None, None),
        P("shard", "rep", None),
        P("shard", "rep", None),
        P("shard", "rep", None),
        P("shard", None, None),
        P("shard", None),
    )
    return jax.shard_map(
        per_device,
        mesh=mesh,
        in_specs=placed,
        out_specs=(P("shard", "rep", None), P("shard", None, None)),
        check_vma=False,
    )
```

profile of v0, /device:TPU:0, one launch (start us, length us, event | category | flops | bytes accessed | tf_op | source)
XLA Modules:
  0.0 74.6 jit_solution(5423783142916893457)
XLA Ops:
  7.2 1.6 %copy.12 = f32[16,1,8,256]{3,0,1,2:T(8,128)} copy(f32[16,1,8,256]{3,2,1,0:T(8,128)} %param.8) | data formatting | bytes 262144 | tf_op args[0]
  8.8 5.2 %all-to-all-start = ((f32[16,1,8,256]{3,0,1,2:T(8,128)}), f32[16,1,8,256]{3,0,1,2:T(8,128)S(1)}, u32[]{:S(2)}, u32[]{:S(2)}) async-start(f32[16,1,8,256]{3,0,1,2:T(8,128)} %copy.12), calls=%async_computation | async-start | bytes 262144 | tf_op jit(solution)/shard_map/all_to_all | solution.py:48
  14.0 0.0 reduce-scatter.2.cloned.1.call-start
  14.0 0.0 copy-start.1
  14.0 0.6 copy-done.1
  14.7 0.1 copy.11
  14.8 0.2 reduce-window.9
  15.0 0.1 reduce.1
  15.1 8.7 %while.14 = (s32[]{:T(128)}, f32[512,128]{1,0:T(8,128)S(1)}, s32[2048]{0:T(1024)}, s32[2048]{0:T(1024)}, s32[128]{0:T(128)S(1)}, /*index=5*/s32[128]{0:T(128)S(1)}, s32[]{:T(128)}, s32[]{:T(128)}, s32[]{:T(128)}, s32[]{:T(128)}) while((s32[]{:T(128)}, f32[512,128]{1,0:T(8,128)S(1)}, s32[2048]{0:T(1024)}, s32[2048]{0:T(1024)}, ...), condition=%wide.region_2.3_spmd.clone, body=%wide.region_1.2_spmd.clone.sunk | while | flops 68223496 | bytes 541873 | solution.py:33
  15.1 0.8 %dynamic_slice.30 = s32[512]{0:T(512)S(1)} dynamic-slice(s32[2048]{0:T(1024)} %get-tuple-element.222, s32[]{:T(128)S(6)} %select_n.28), dynamic_slice_sizes={512} | dynamic-slice | bytes 4100 | tf_op jit(solution)/shard_map/while/body/eval_jaxpr/dynamic_slice | solution.py:21
  15.9 0.8 %dynamic_slice.31 = s32[512]{0:T(512)S(1)} dynamic-slice(s32[2048]{0:T(1024)} %get-tuple-element.221, s32[]{:T(128)S(6)} %select_n.28), dynamic_slice_sizes={512} | dynamic-slice | bytes 4100 | tf_op jit(solution)/shard_map/while/body/eval_jaxpr/dynamic_slice | solution.py:20
  16.6 0.6 convolution_add_fusion.2
  17.3 0.8 %dynamic_slice.30 = s32[512]{0:T(512)S(1)} dynamic-slice(s32[2048]{0:T(1024)} %get-tuple-element.222, s32[]{:T(128)S(6)} %select_n.28), dynamic_slice_sizes={512} | dynamic-slice | bytes 4100 | tf_op jit(solution)/shard_map/while/body/eval_jaxpr/dynamic_slice | solution.py:21
  18.0 0.8 %dynamic_slice.31 = s32[512]{0:T(512)S(1)} dynamic-slice(s32[2048]{0:T(1024)} %get-tuple-element.221, s32[]{:T(128)S(6)} %select_n.28), dynamic_slice_sizes={512} | dynamic-slice | bytes 4100 | tf_op jit(solution)/shard_map/while/body/eval_jaxpr/dynamic_slice | solution.py:20
  18.8 0.6 convolution_add_fusion.2
  19.4 0.8 %dynamic_slice.30 = s32[512]{0:T(512)S(1)} dynamic-slice(s32[2048]{0:T(1024)} %get-tuple-element.222, s32[]{:T(128)S(6)} %select_n.28), dynamic_slice_sizes={512} | dynamic-slice | bytes 4100 | tf_op jit(solution)/shard_map/while/body/eval_jaxpr/dynamic_slice | solution.py:21
  20.2 0.8 %dynamic_slice.31 = s32[512]{0:T(512)S(1)} dynamic-slice(s32[2048]{0:T(1024)} %get-tuple-element.221, s32[]{:T(128)S(6)} %select_n.28), dynamic_slice_sizes={512} | dynamic-slice | bytes 4100 | tf_op jit(solution)/shard_map/while/body/eval_jaxpr/dynamic_slice | solution.py:20
  21.0 0.6 convolution_add_fusion.2
  21.6 0.8 %dynamic_slice.30 = s32[512]{0:T(512)S(1)} dynamic-slice(s32[2048]{0:T(1024)} %get-tuple-element.222, s32[]{:T(128)S(6)} %select_n.28), dynamic_slice_sizes={512} | dynamic-slice | bytes 4100 | tf_op jit(solution)/shard_map/while/body/eval_jaxpr/dynamic_slice | solution.py:21
  22.4 0.8 %dynamic_slice.31 = s32[512]{0:T(512)S(1)} dynamic-slice(s32[2048]{0:T(1024)} %get-tuple-element.221, s32[]{:T(128)S(6)} %select_n.28), dynamic_slice_sizes={512} | dynamic-slice | bytes 4100 | tf_op jit(solution)/shard_map/while/body/eval_jaxpr/dynamic_slice | solution.py:20
  23.1 0.6 convolution_add_fusion.2
  23.8 0.0 all-to-all-done
  23.8 1.4 %fusion.12 = f32[1,512,256]{2,1,0:T(8,128)} fusion(f32[512,128]{1,0:T(8,128)S(1)} %get-tuple-element.126, f32[128,256]{1,0:T(8,128)S(1)} %bitcast.24), kind=kOutput, calls=%fused_computation.16 | convolution fusion | flops 201457664 | bytes 917504 | tf_op jit(solution)/shard_map/dot_general | solution.py:35
  25.1 0.0 reduce-scatter.2.cloned.1.call-update
  25.2 23.7 %reduce-scatter.2.cloned.1.call-done = f32[1,128,256]{2,1,0:T(8,128)} async-done(((f32[1,512,256]{2,1,0:T(8,128)}), f32[1,128,256]{2,1,0:T(8,128)}) %reduce-scatter.2.cloned.1.call-update) | async-done | bytes 131088 | tf_op jit(solution)/shard_map/reduce_scatter | solution.py:56
  48.8 0.0 copy-start
  48.8 1.1 %multiply_reduce_fusion = f32[128]{0:T(128)S(1)} fusion(f32[1,128,256]{2,1,0:T(8,128)} %reduce-scatter.2.cloned.1.call-done), kind=kLoop, calls=%fused_computation.18 | loop fusion | flops 65408 | bytes 131584 | tf_op jit(solution)/shard_map/reduce_sum | solution.py:43
  49.9 0.7 fusion.15
  50.6 0.0 copy-done
  50.6 1.0 %divide_subtract_fusion = f32[1,128,256]{2,1,0:T(8,128)S(1)} fusion(f32[1,128,256]{2,1,0:T(8,128)S(1)} %copy-done, f32[1,512,256]{2,1,0:T(8,128)} %param.12, s32[]{:T(128)S(6)} %select_n.20, f32[128]{0:T(128)S(1)} %fusion.15), kind=kLoop, calls=%fused_computation.17 | loop fusion | flops 98304 | bytes 393732 | tf_op jit(solution)/shard_map/sub | solution.py:44
  51.6 15.3 %all_gather.3 = f32[1,512,256]{2,1,0:T(8,128)S(1)} all-gather(f32[1,128,256]{2,1,0:T(8,128)S(1)} %divide_subtract_fusion), channel_id=1, replica_groups=mesh['shard'=8,'rep'=4] {'rep'}, dimensions={1}, use_global_device_ids=true | all-gather | bytes 655360 | tf_op jit(solution)/shard_map/all_gather | solution.py:60
  66.9 0.8 %copy.20 = f32[1,512,256]{2,1,0:T(8,128)} copy(f32[1,512,256]{2,1,0:T(8,128)S(1)} %all_gather.3) | data formatting | bytes 1048576
  (6 shorter events, 0.0 us)
Async XLA Ops:
  8.8 15.0 %all-to-all-start = ((f32[16,1,8,256]{3,0,1,2:T(8,128)}), f32[16,1,8,256]{3,0,1,2:T(8,128)S(1)}, u32[]{:S(2)}, u32[]{:S(2)}) async-start(f32[16,1,8,256]{3,0,1,2:T(8,128)} %copy.12), calls=%async_computation | async-start | bytes 262144 | tf_op jit(solution)/shard_map/all_to_all | solution.py:48
  14.0 34.9 %reduce-scatter.2.cloned.1.call-start = ((), (), s32[]{:S(2)}) async-start(), calls=%async_computation.2 | async-start | bytes 655360 | tf_op jit(solution)/shard_map/reduce_scatter | solution.py:56
  14.0 0.7 copy-start.1
  48.8 1.8 %copy-start = (f32[1,128,256]{2,1,0:T(8,128)S(1)}, f32[1,128,256]{2,1,0:T(8,128)}, u32[]{:S(2)}) copy-start(f32[1,128,256]{2,1,0:T(8,128)} %reduce-scatter.2.cloned.1.call-done) | copy-start | bytes 393220
Sparse Core Ops, SparseCore 0:
  25.3 23.5 reduce-scatter.1
where the time goes:
time: 75.2 us; the launch traced here: 74.6 us
  waiting for transfers between devices  23.7 us (32%)
  blocking collectives  15.3 us (20%)
  between operations  14.1 us (19%)
  local copies, waits for them, and re-layouts  9.26 us (12%)
  starting transfers between devices  5.23 us (7%)
  matrix products  3.76 us (5%)
  other arithmetic  3.04 us (4%)
    reduce_scatter x1, waiting for transfers between devices, per_device(): grad_part = lax.psum_scatter(local, 'rep', scatter_dimension=1, tiled=True)  23.7 us
    all_gather x1, blocking collectives, per_device(): updated = lax.all_gather(fresh, 'rep', axis=1, tiled=True)  15.3 us
    all_to_all x1, starting transfers between devices, per_device(): lax.all_to_all(pooled_grad, 'shard', split_axis=2, concat_axis=0, tiled=T...  5.2 us
    dynamic_slice x4, local copies, waits for them, and re-layouts, add_block(): factor = lax.dynamic_slice_in_dim(weights, start, span)  3.06 us
    unnamed x6, local copies, waits for them, and re-layouts  3.05 us
    dynamic_slice x4, local copies, waits for them, and re-layouts, add_block(): target = lax.dynamic_slice_in_dim(slots, start, span)  3.04 us
    dot_general x4, matrix products, add_block(): lax.dot_general(chosen, member, (((0,), (0,)), ((), ())), preferred_eleme...  2.4 us
  transfers between devices with their start and end apart: 2, of which 1 were waited for; matrix products, arithmetic and copies ran while one was open for 12% of the time, Pallas kernels for 0%

commit v1 on v0

--- a/solution.py
+++ b/solution.py
@@ -4,6 +4,17 @@
 from jax.sharding import PartitionSpec as P
 
 learn_rate = 0.5
+
+
+def split_up(value, dim, size):
+    before, after = (value.shape[:dim], value.shape[dim + 1 :])
+    return jnp.moveaxis(value.reshape(*before, size, -1, *after), dim, 0)
+
+
+def in_order(parts, dim):
+    parts = jnp.moveaxis(parts, 0, dim)
+    lengths = parts.shape
+    return parts.reshape(*lengths[:dim], lengths[dim] * lengths[dim + 1], *lengths[dim + 2 :])
 
 
 def table_rows(arrived, lengths, slots, weights, height):
@@ -45,7 +56,15 @@
 
 
 def per_device(pooled_grad, bag_lengths, row_slots, id_weights, touched_rows, accumulator):
-    arrived = lax.all_to_all(pooled_grad, "shard", split_axis=2, concat_axis=0, tiled=True)
+    size, here = (lax.axis_size("shard"), lax.axis_index("shard"))
+    blocks = split_up(pooled_grad, 2, size)
+    result = blocks
+    for step_2 in range(1, size):
+        target_2, source = ((here + step_2) % size, (here - step_2) % size)
+        sent = lax.dynamic_index_in_dim(blocks, target_2, 0)
+        received = lax.ppermute(sent, "shard", [(i, (i + step_2) % size) for i in range(size)])
+        result = lax.dynamic_update_slice_in_dim(result, received, source, axis=0)
+    arrived = in_order(result, 0)
     height = touched_rows.shape[1]
     owned = touched_rows.shape[0]
     local = jnp.stack(

time: 75.2 us -> 81.9 us (1.089)
  waiting for transfers between devices: 23.7 us -> 29.3 us
  starting transfers between devices: 5.23 us -> 6.84 us
    ppermute x0 -> x7, waiting for transfers between devices: none -> 7.89 us  [per_device(): lax.ppermute(sent, 'shard', [(i, (i + step_2) % size) for i in range(size)])]
    ppermute x0 -> x7, starting transfers between devices: none -> 6.8 us  [per_device(): lax.ppermute(sent, 'shard', [(i, (i + step_2) % size) for i in range(size)])]
    all_to_all x1 -> x0, starting transfers between devices: 5.2 us -> none  [per_device(): lax.all_to_all(pooled_grad, 'shard', split_axis=2, concat_axis=0, tiled=T...]
    reduce_scatter x1, waiting for transfers between devices: 23.7 us -> 21.4 us  [per_device(): grad_part = lax.psum_scatter(local, 'rep', scatter_dimension=1, tiled=True)]
    unnamed x6 -> x8, local copies, waits for them, and re-layouts: 3.05 us -> 2.26 us
  transfers between devices with their start and end apart: 2 -> 8, of which waited for: 1 -> 3; matrix products, arithmetic and copies ran while one was open for 12% -> 11% of each run, Pallas kernels for 0% -> 0%
where the time goes in v1:
time: 81.9 us; the launch traced here: 81.5 us
  waiting for transfers between devices  29.3 us (36%)
  blocking collectives  15.5 us (19%)
  between operations  14.4 us (18%)
  local copies, waits for them, and re-layouts  8.53 us (10%)
  starting transfers between devices  6.84 us (8%)
  matrix products  3.76 us (5%)
  other arithmetic  3.04 us (4%)
    reduce_scatter x1, waiting for transfers between devices, per_device(): grad_part = lax.psum_scatter(local, 'rep', scatter_dimension=1, tiled=True)  21.4 us
    all_gather x1, blocking collectives, per_device(): updated = lax.all_gather(fresh, 'rep', axis=1, tiled=True)  15.5 us
    ppermute x7, waiting for transfers between devices, per_device(): lax.ppermute(sent, 'shard', [(i, (i + step_2) % size) for i in range(size)])  7.89 us
    ppermute x7, starting transfers between devices, per_device(): lax.ppermute(sent, 'shard', [(i, (i + step_2) % size) for i in range(size)])  6.8 us
    dynamic_slice x4, local copies, waits for them, and re-layouts, add_block(): factor = lax.dynamic_slice_in_dim(weights, start, span)  3.06 us
    dynamic_slice x4, local copies, waits for them, and re-layouts, add_block(): target = lax.dynamic_slice_in_dim(slots, start, span)  3.04 us
    dot_general x4, matrix products, add_block(): lax.dot_general(chosen, member, (((0,), (0,)), ((), ())), preferred_eleme...  2.4 us
    unnamed x8, local copies, waits for them, and re-layouts  2.26 us
  transfers between devices with their start and end apart: 8, of which 3 were waited for; matrix products, arithmetic and copies ran while one was open for 11% of the time, Pallas kernels for 0%

profile of v1, /device:TPU:0, one launch (start us, length us, event | category | flops | bytes accessed | tf_op | source)
XLA Modules:
  0.0 81.5 jit_solution(2180782518432887381)
XLA Ops:
  7.2 0.0 copy-start.1
  7.2 0.0 reduce-scatter.2.cloned.1.call-start
  7.3 0.8 copy-done.1
  8.2 3.4 %collective-permute-start.6 = (f32[1,16,1,1,256]{4,1,3,2,0:T(8,128)S(1)}, f32[1,16,1,1,256]{4,1,3,2,0:T(8,128)S(1)}, u32[]{:S(2)}, u32[]{:S(2)}) collective-permute-start(f32[1,16,1,1,256]{4,1,3,2,0:T(8,128)S(1)} %get-tuple-element.162), channel_id=1, source_target_pairs={{0,28},{4,0},{8,4},{12,8},{16,12},{20,16},{24,20},{28,24},{1,29},{... | collective-permute-start | bytes 49160 | tf_op jit(solution)/shard_map/ppermute | solution.py:65
  11.6 0.6 collective-permute-start.5
  12.2 0.3 collective-permute-start.4
  12.5 1.5 %collective-permute-start.3 = (f32[1,16,1,1,256]{4,1,3,2,0:T(8,128)S(1)}, f32[1,16,1,1,256]{4,1,3,2,0:T(8,128)S(1)}, u32[]{:S(2)}, u32[]{:S(2)}) collective-permute-start(f32[1,16,1,1,256]{4,1,3,2,0:T(8,128)S(1)} %get-tuple-element.165), channel_id=1, source_target_pairs={{0,16},{4,20},{8,24},{12,28},{16,0},{20,4},{24,8},{28,12},{1,17},{... | collective-permute-start | bytes 49160 | tf_op jit(solution)/shard_map/ppermute | solution.py:65
  14.0 0.9 %collective-permute-start = (f32[1,16,1,1,256]{4,1,3,2,0:T(8,128)S(1)}, f32[1,16,1,1,256]{4,1,3,2,0:T(8,128)S(1)}, u32[]{:S(2)}, u32[]{:S(2)}) collective-permute-start(f32[1,16,1,1,256]{4,1,3,2,0:T(8,128)S(1)} %get-tuple-element.168), channel_id=1, source_target_pairs={{0,4},{4,8},{8,12},{12,16},{16,20},{20,24},{24,28},{28,0},{1,5},{5... | collective-permute-start | bytes 49160 | tf_op jit(solution)/shard_map/ppermute | solution.py:65
  14.9 0.0 copy-start.2
  14.9 0.7 copy-done.2
  15.6 0.1 copy.11
  15.7 0.2 reduce-window.9
  15.9 0.1 reduce.1
  16.0 8.7 %while.14 = (s32[]{:T(128)}, f32[512,128]{1,0:T(8,128)S(1)}, s32[2048]{0:T(1024)}, s32[2048]{0:T(1024)}, s32[128]{0:T(128)S(1)}, /*index=5*/s32[128]{0:T(128)S(1)}, s32[]{:T(128)}, s32[]{:T(128)}, s32[]{:T(128)}, s32[]{:T(128)}) while((s32[]{:T(128)}, f32[512,128]{1,0:T(8,128)S(1)}, s32[2048]{0:T(1024)}, s32[2048]{0:T(1024)}, ...), condition=%wide.region_2.3_spmd.clone, body=%wide.region_1.2_spmd.clone.sunk | while | flops 68223496 | bytes 541873 | solution.py:44
  16.0 0.8 dynamic_slice.63
  16.8 0.8 dynamic_slice.64
  17.5 0.6 convolution_add_fusion.2
  18.2 0.8 dynamic_slice.63
  18.9 0.8 dynamic_slice.64
  19.7 0.6 convolution_add_fusion.2
  20.3 0.8 dynamic_slice.63
  21.1 0.8 dynamic_slice.64
  21.9 0.6 convolution_add_fusion.2
  22.5 0.8 dynamic_slice.63
  23.3 0.8 dynamic_slice.64
  24.0 0.6 convolution_add_fusion.2
  24.8 0.0 collective-permute-done
  24.8 0.1 collective-permute-start.1
  24.9 4.6 %collective-permute-done.1 = f32[1,16,1,1,256]{4,1,3,2,0:T(8,128)S(1)} collective-permute-done((f32[1,16,1,1,256]{4,1,3,2,0:T(8,128)S(1)}, f32[1,16,1,1,256]{4,1,3,2,0:T(8,128)S(1)}, u32[]{:S(2)}, u32[]{:S(2)}) %collective-permute-start.1) | collective-permute-done | bytes 16416 | tf_op jit(solution)/shard_map/ppermute | solution.py:65
  29.5 0.0 collective-permute-start.2
  29.5 3.3 %collective-permute-done.2 = f32[1,16,1,1,256]{4,1,3,2,0:T(8,128)S(1)} collective-permute-done((f32[1,16,1,1,256]{4,1,3,2,0:T(8,128)S(1)}, f32[1,16,1,1,256]{4,1,3,2,0:T(8,128)S(1)}, u32[]{:S(2)}, u32[]{:S(2)}) %collective-permute-start.2) | collective-permute-done | bytes 16416 | tf_op jit(solution)/shard_map/ppermute | solution.py:65
  32.8 0.0 collective-permute-done.3
  32.8 0.0 collective-permute-done.4
  32.8 0.0 collective-permute-done.5
  32.8 0.0 collective-permute-done.6
  32.9 1.4 %fusion.12 = f32[1,512,256]{2,1,0:T(8,128)} fusion(f32[512,128]{1,0:T(8,128)S(1)} %get-tuple-element.126, f32[128,256]{1,0:T(8,128)S(1)} %bitcast.49), kind=kOutput, calls=%fused_computation.16 | convolution fusion | flops 201457664 | bytes 917504 | tf_op jit(solution)/shard_map/dot_general | solution.py:46
  34.2 0.0 reduce-scatter.2.cloned.1.call-update
  34.3 21.4 %reduce-scatter.2.cloned.1.call-done = f32[1,128,256]{2,1,0:T(8,128)} async-done(((f32[1,512,256]{2,1,0:T(8,128)}), f32[1,128,256]{2,1,0:T(8,128)}) %reduce-scatter.2.cloned.1.call-update) | async-done | bytes 131088 | tf_op jit(solution)/shard_map/reduce_scatter | solution.py:75
  55.6 0.0 copy-start
  55.6 1.1 %multiply_reduce_fusion = f32[128]{0:T(128)S(1)} fusion(f32[1,128,256]{2,1,0:T(8,128)} %reduce-scatter.2.cloned.1.call-done), kind=kLoop, calls=%fused_computation.18 | loop fusion | flops 65408 | bytes 131584 | tf_op jit(solution)/shard_map/reduce_sum | solution.py:54
  56.7 0.7 add_bitcast_fusion
  57.4 0.0 copy-done
  57.4 1.0 %divide_subtract_fusion = f32[1,128,256]{2,1,0:T(8,128)S(1)} fusion(f32[1,128,256]{2,1,0:T(8,128)S(1)} %copy-done, f32[1,512,256]{2,1,0:T(8,128)} %param.12, s32[]{:T(128)S(6)} %select_n.150, f32[128]{0:T(128)S(1)} %add_bitcast_fusion), kind=kLoop, calls=%fused_computation.17 | loop fusion | flops 98304 | bytes 393732 | tf_op jit(solution)/shard_map/sub | solution.py:55
  58.4 15.5 %all_gather.3 = f32[1,512,256]{2,1,0:T(8,128)S(1)} all-gather(f32[1,128,256]{2,1,0:T(8,128)S(1)} %divide_subtract_fusion), channel_id=1, replica_groups=mesh['shard'=8,'rep'=4] {'rep'}, dimensions={1}, use_global_device_ids=true | all-gather | bytes 655360 | tf_op jit(solution)/shard_map/all_gather | solution.py:79
  73.8 0.8 copy.44
  (15 shorter events, 0.1 us)
Async XLA Ops:
  7.2 0.9 %copy-start.1 = (f32[16,1,8,256]{3,2,1,0:T(8,128)S(1)}, f32[16,1,8,256]{3,2,1,0:T(8,128)}, u32[]{:S(2)}) copy-start(f32[16,1,8,256]{3,2,1,0:T(8,128)} %param.8) | copy-start | bytes 393220
  7.2 48.4 %reduce-scatter.2.cloned.1.call-start = ((), (), s32[]{:S(2)}) async-start(), calls=%async_computation.1 | async-start | bytes 655360 | tf_op jit(solution)/shard_map/reduce_scatter | solution.py:75
  8.2 24.7 %collective-permute-start.6 = (f32[1,16,1,1,256]{4,1,3,2,0:T(8,128)S(1)}, f32[1,16,1,1,256]{4,1,3,2,0:T(8,128)S(1)}, u32[]{:S(2)}, u32[]{:S(2)}) collective-permute-start(f32[1,16,1,1,256]{4,1,3,2,0:T(8,128)S(1)} %get-tuple-element.162), channel_id=1, source_target_pairs={{0,28},{4,0},{8,4},{12,8},{16,12},{20,16},{24,20},{28,24},{1,29},{... | collective-permute-start | bytes 49160 | tf_op jit(solution)/shard_map/ppermute | solution.py:65
  11.6 21.2 %collective-permute-start.5 = (f32[1,16,1,1,256]{4,1,3,2,0:T(8,128)S(1)}, f32[1,16,1,1,256]{4,1,3,2,0:T(8,128)S(1)}, u32[]{:S(2)}, u32[]{:S(2)}) collective-permute-start(f32[1,16,1,1,256]{4,1,3,2,0:T(8,128)S(1)} %get-tuple-element.163), channel_id=1, source_target_pairs={{0,24},{4,28},{8,0},{12,4},{16,8},{20,12},{24,16},{28,20},{1,25},{... | collective-permute-start | bytes 49160 | tf_op jit(solution)/shard_map/ppermute | solution.py:65
  12.2 20.6 %collective-permute-start.4 = (f32[1,16,1,1,256]{4,1,3,2,0:T(8,128)S(1)}, f32[1,16,1,1,256]{4,1,3,2,0:T(8,128)S(1)}, u32[]{:S(2)}, u32[]{:S(2)}) collective-permute-start(f32[1,16,1,1,256]{4,1,3,2,0:T(8,128)S(1)} %get-tuple-element.164), channel_id=1, source_target_pairs={{0,20},{4,24},{8,28},{12,0},{16,4},{20,8},{24,12},{28,16},{1,21},{... | collective-permute-start | bytes 49160 | tf_op jit(solution)/shard_map/ppermute | solution.py:65
  12.5 20.3 %collective-permute-start.3 = (f32[1,16,1,1,256]{4,1,3,2,0:T(8,128)S(1)}, f32[1,16,1,1,256]{4,1,3,2,0:T(8,128)S(1)}, u32[]{:S(2)}, u32[]{:S(2)}) collective-permute-start(f32[1,16,1,1,256]{4,1,3,2,0:T(8,128)S(1)} %get-tuple-element.165), channel_id=1, source_target_pairs={{0,16},{4,20},{8,24},{12,28},{16,0},{20,4},{24,8},{28,12},{1,17},{... | collective-permute-start | bytes 49160 | tf_op jit(solution)/shard_map/ppermute | solution.py:65
  14.0 10.8 %collective-permute-start = (f32[1,16,1,1,256]{4,1,3,2,0:T(8,128)S(1)}, f32[1,16,1,1,256]{4,1,3,2,0:T(8,128)S(1)}, u32[]{:S(2)}, u32[]{:S(2)}) collective-permute-start(f32[1,16,1,1,256]{4,1,3,2,0:T(8,128)S(1)} %get-tuple-element.168), channel_id=1, source_target_pairs={{0,4},{4,8},{8,12},{12,16},{16,20},{20,24},{24,28},{28,0},{1,5},{5... | collective-permute-start | bytes 49160 | tf_op jit(solution)/shard_map/ppermute | solution.py:65
  14.9 0.7 copy-start.2
  24.8 4.7 %collective-permute-start.1 = (f32[1,16,1,1,256]{4,1,3,2,0:T(8,128)S(1)}, f32[1,16,1,1,256]{4,1,3,2,0:T(8,128)S(1)}, u32[]{:S(2)}, u32[]{:S(2)}) collective-permute-start(f32[1,16,1,1,256]{4,1,3,2,0:T(8,128)S(1)} %get-tuple-element.167), channel_id=1, source_target_pairs={{0,8},{4,12},{8,16},{12,20},{16,24},{20,28},{24,0},{28,4},{1,9},{5... | collective-permute-start | bytes 49160 | tf_op jit(solution)/shard_map/ppermute | solution.py:65
  29.5 3.3 %collective-permute-start.2 = (f32[1,16,1,1,256]{4,1,3,2,0:T(8,128)S(1)}, f32[1,16,1,1,256]{4,1,3,2,0:T(8,128)S(1)}, u32[]{:S(2)}, u32[]{:S(2)}) collective-permute-start(f32[1,16,1,1,256]{4,1,3,2,0:T(8,128)S(1)} %get-tuple-element.166), channel_id=1, source_target_pairs={{0,12},{4,16},{8,20},{12,24},{16,28},{20,0},{24,4},{28,8},{1,13},{... | collective-permute-start | bytes 49160 | tf_op jit(solution)/shard_map/ppermute | solution.py:65
  55.6 1.8 %copy-start = (f32[1,128,256]{2,1,0:T(8,128)S(1)}, f32[1,128,256]{2,1,0:T(8,128)}, u32[]{:S(2)}) copy-start(f32[1,128,256]{2,1,0:T(8,128)} %reduce-scatter.2.cloned.1.call-done) | copy-start | bytes 393220
Sparse Core Ops, SparseCore 0:
  34.4 21.1 reduce-scatter.1
